TPU v7x, 512 devices: a whole 4x4x16 slice. The times are simulated.
512 devices in a mesh: gx: 16 (over z_hi, y, core), gy: 32 (over z_lo, x).
Axes of the slice: x: 4, y: 4, z: 16 (z_hi: 2, z_lo: 8; z = z_hi * 8 + z_lo), core: 2. Of those that a mesh axis runs over, the one named last changes fastest.
Arguments:
- adjoint_in: float32 [19, 256, 4, 4096], P(None, 'gx', None, 'gy'), may hold values from -6 to 6
- velocity: bfloat16 [2, 3, 256, 4, 4096], P(None, None, 'gx', None, 'gy')
- solid_tiles: int32 [64, 4, 1024], P('gx', None, 'gy'), may hold values from 0 to 1, as said below
- link_blocked: int32 [18, 256, 4, 4096], P(None, 'gx', None, 'gy'), may hold values from 0 to 1, as said below
Outputs:
- adjoint_out: float32 [19, 256, 4, 4096], P(None, 'gx', None, 'gy')
- drag_sens: float32 [1], replicated
Inputs may be any that keep to these rules, and one draw needn't show every extreme that they name: `solid_tiles`: 1 on the levels below a tile's building height, heights 0 to 3 per tile. `link_blocked`: entry i - 1 is 1 exactly where the cell x + c_i (periodic in the plane) is solid or lies outside the 4 levels.
All inputs are finite; a program needn't handle non-finite values.
Results may differ from a plain program's by a relative error of at most 0.0003.
Values sent between devices are 32-bit elements; how exact they have to be, the bound alone decides.
A program may use at most 64 MiB of HBM per device.

v0:
```python
import math
import jax
import jax.numpy as jnp
from jax import lax
from jax.sharding import PartitionSpec as P

TILE = 4
STEPS = 2
lattice_speeds = (
    (0, 0, 0),
    (1, 0, 0),
    (-1, 0, 0),
    (0, 1, 0),
    (0, -1, 0),
    (0, 0, 1),
    (0, 0, -1),
    (1, 1, 0),
    (-1, -1, 0),
    (1, -1, 0),
    (-1, 1, 0),
    (1, 0, 1),
    (-1, 0, -1),
    (1, 0, -1),
    (-1, 0, 1),
    (0, 1, 1),
    (0, -1, -1),
    (0, 1, -1),
    (0, -1, 1),
)
lattice_weights = (1.0 / 3.0,) + (1.0 / 18.0,) * 6 + (1.0 / 36.0,) * 12
relax_rate = 1.6
drag_factor = 20.0


def with_halo(block, sides, width):
    for axis, dim in sides:
        count = lax.axis_size(axis)
        forward = [(i, i + 1) for i in range(count - 1)]
        forward.append((count - 1, 0))
        backward = [(target, source) for source, target in forward]
        low = lax.ppermute(
            lax.slice_in_dim(block, block.shape[dim] - width, None, axis=dim), axis, forward
        )
        high = lax.ppermute(lax.slice_in_dim(block, 0, width, axis=dim), axis, backward)
        block = jnp.concatenate([low, block, high], axis=dim)
    return block


def opposite_of(number):
    return number + 1 if number % 2 == 1 else number - 1


def shift_level(field, lift):
    if lift == 1:
        return jnp.concatenate([field[:, 1:], jnp.zeros_like(field[:, :1])], axis=1)
    if lift == -1:
        return jnp.concatenate([jnp.zeros_like(field[:, :1]), field[:, :-1]], axis=1)
    return field


def adjoint_collide(moved, flow, fluid):
    speed_sq = flow[0] * flow[0] + flow[1] * flow[1] + flow[2] * flow[2]
    scalar_part = jnp.zeros_like(speed_sq)
    vector_part = [jnp.zeros_like(speed_sq) for axis_number in range(3)]
    drag_local = jnp.zeros_like(speed_sq)
    for number in range(19):
        speed = lattice_speeds[number]
        along = speed[0] * flow[0] + speed[1] * flow[1] + speed[2] * flow[2]
        weighted = lattice_weights[number] * moved[number]
        scalar_part = scalar_part + weighted * (
            1.0 + 3.0 * along + 4.5 * along * along - 1.5 * speed_sq
        )
        for axis_number in range(3):
            vector_part[axis_number] = vector_part[axis_number] + weighted * (
                3.0 * speed[axis_number]
                + 9.0 * along * speed[axis_number]
                - 3.0 * flow[axis_number]
            )
        drag_local = drag_local + 3.0 * weighted * along
    results = []
    for number in range(19):
        speed = lattice_speeds[number]
        projected = scalar_part
        for axis_number in range(3):
            projected = projected + vector_part[axis_number] * (
                speed[axis_number] - flow[axis_number]
            )
        results.append(fluid * ((1.0 - relax_rate) * moved[number] + relax_rate * projected))
    return (jnp.stack(results), fluid * drag_local)


def stream_back(padded, centre, blocked, span_x, span_y):
    moved = [centre[0]]
    for number in range(1, 19):
        speed = lattice_speeds[number]
        source = padded[
            number, 1 + speed[0] : 1 + speed[0] + span_x, :, 1 + speed[1] : 1 + speed[1] + span_y
        ]
        source = shift_level(source, speed[2])
        bounced = centre[opposite_of(number)] + 2.0 * speed[0]
        moved.append(jnp.where(blocked[number - 1] == 1, bounced, source))
    return moved


def per_device(adjoint_in, velocity, solid_tiles, link_blocked):
    rows_x = adjoint_in.shape[1]
    rows_y = adjoint_in.shape[3]
    levels = adjoint_in.shape[2]
    solid = jnp.repeat(jnp.repeat(solid_tiles, TILE, axis=0), TILE, axis=2)
    fluid = 1.0 - solid.astype(jnp.float32)
    state = adjoint_in
    step_terms = []
    for adjoint_step in range(STEPS):
        flow = velocity[adjoint_step].astype(jnp.float32)
        padded = with_halo(state, (("gx", 1), ("gy", 3)), 1)
        moved = stream_back(padded, state, link_blocked, rows_x, rows_y)
        state, drag_field = adjoint_collide(moved, flow, fluid)
        step_terms.append(jnp.sum(drag_field))
    total = jnp.zeros((), jnp.float32)
    for adjoint_step in range(STEPS):
        total = total + lax.psum(step_terms[adjoint_step], ("gx", "gy"))
    cell_count = rows_x * lax.axis_size("gx") * rows_y * lax.axis_size("gy") * levels
    scale = drag_factor / math.sqrt(cell_count)
    return (state, (-scale * total).reshape(1))


def solution(mesh):
    placed = (
        P(None, "gx", None, "gy"),
        P(None, None, "gx", None, "gy"),
        P("gx", None, "gy"),
        P(None, "gx", None, "gy"),
    )
    return jax.shard_map(
        per_device,
        mesh=mesh,
        in_specs=placed,
        out_specs=(P(None, "gx", None, "gy"), P()),
        check_vma=False,
    )
```

profile of v0, /device:TPU:1, one launch (start us, length us, event | category | flops | bytes accessed | tf_op | source)
XLA Modules:
  0.0 222.9 jit_solution(16425646416944457608)
XLA Ops:
  0.6 0.8 fusion.265
  1.4 4.6 %collective-permute-start.1 = (f32[19,1,4,128]{3,2,1,0:T(4,128)S(1)}, f32[19,1,4,128]{3,2,1,0:T(4,128)S(1)}, u32[]{:S(2)}, u32[]{:S(2)}) collective-permute-start(f32[19,1,4,128]{3,2,1,0:T(4,128)S(1)} %get-tuple-element.193), channel_id=1, source_target_pairs={{0,32},{32,64},{64,96},{96,128},{128,160},{160,192},{192,224},{224... | collective-permute-start | bytes 116744 | tf_op jit(solution)/shard_map/ppermute | solution.py:41
  6.0 6.2 %collective-permute-start = (f32[19,1,4,128]{3,2,1,0:T(4,128)S(1)}, f32[19,1,4,128]{3,2,1,0:T(4,128)S(1)}, u32[]{:S(2)}, u32[]{:S(2)}) collective-permute-start(f32[19,1,4,128]{3,2,1,0:T(4,128)S(1)} %get-tuple-element.194), channel_id=1, source_target_pairs={{32,0},{64,32},{96,64},{128,96},{160,128},{192,160},{224,192},{256... | collective-permute-start | bytes 116744 | tf_op jit(solution)/shard_map/ppermute | solution.py:44
  12.3 1.7 fusion.264
  14.1 0.8 fusion.266
  15.0 0.6 copy-done.67
  15.9 0.6 slice.360
  16.5 0.6 slice.361
  17.6 0.6 fusion.262
  18.3 0.6 fusion.261
  20.4 10.9 %collective-permute-start.2 = (f32[19,18,4,1]{0,2,3,1:T(4,128)S(1)}, f32[19,18,4,1]{0,2,3,1:T(4,128)}, u32[]{:S(2)}, u32[]{:S(2)}) collective-permute-start(f32[19,18,4,1]{0,2,3,1:T(4,128)S(1)} %copy.538), channel_id=1, source_target_pairs={{1,0},{2,1},{3,2},{4,3},{5,4},{6,5},{7,6},{8,7},{9,8},{10,9},{11,1... | collective-permute-start | bytes 16424 | tf_op jit(solution)/shard_map/ppermute | solution.py:44
  31.3 1.9 collective-permute-start.3
  33.3 0.6 slice.367
  33.9 0.6 slice.363
  34.5 0.6 slice.369
  35.2 0.6 slice.365
  35.8 8.9 %collective-permute-done.3 = f32[19,18,4,1]{0,2,3,1:T(4,128)S(1)} collective-permute-done((f32[19,18,4,1]{0,2,3,1:T(4,128)S(1)}, f32[19,18,4,1]{0,2,3,1:T(4,128)S(1)}, u32[]{:S(2)}, u32[]{:S(2)}) %collective-permute-start.3) | collective-permute-done | bytes 5504 | tf_op jit(solution)/shard_map/ppermute | solution.py:41
  44.7 1.0 copy.442
  45.7 1.8 copy.438
  48.9 1.7 multiply_reduce_fusion.1
  51.4 0.6 constant_dynamic-update-slice_fusion.17
  52.0 0.6 constant_dynamic-update-slice_fusion.16
  52.6 0.6 constant_dynamic-update-slice_fusion.15
  53.2 0.6 constant_dynamic-update-slice_fusion.14
  53.9 0.6 constant_dynamic-update-slice_fusion.13
  54.5 0.6 constant_dynamic-update-slice_fusion.12
  55.1 0.6 constant_dynamic-update-slice_fusion.11
  55.8 0.6 constant_dynamic-update-slice_fusion.10
  56.4 0.6 constant_dynamic-update-slice_fusion.9
  57.0 0.6 constant_dynamic-update-slice_fusion.8
  57.6 0.6 constant_dynamic-update-slice_fusion.7
  58.3 14.7 %collective-permute-start.4 = (f32[19,1,4,128]{3,2,1,0:T(4,128)S(1)}, f32[19,1,4,128]{3,2,1,0:T(4,128)S(1)}, u32[]{:S(2)}, u32[]{:S(2)}) collective-permute-start(f32[19,1,4,128]{3,2,1,0:T(4,128)S(1)} %bitcast.557), channel_id=1, source_target_pairs={{32,0},{64,32},{96,64},{128,96},{160,128},{192,160},{224,192},{256... | collective-permute-start | bytes 116744 | tf_op jit(solution)/shard_map/ppermute | solution.py:44
  73.0 1.9 collective-permute-start.5
  75.0 0.6 slice.382
  75.6 0.6 slice.381
  76.2 6.9 %collective-permute-done.5 = f32[19,1,4,128]{3,2,1,0:T(4,128)S(1)} collective-permute-done((f32[19,1,4,128]{3,2,1,0:T(4,128)S(1)}, f32[19,1,4,128]{3,2,1,0:T(4,128)S(1)}, u32[]{:S(2)}, u32[]{:S(2)}) %collective-permute-start.5) | collective-permute-done | bytes 38944 | tf_op jit(solution)/shard_map/ppermute | solution.py:41
  83.6 0.6 copy.504
  84.8 3.1 %collective-permute-start.6 = (f32[19,18,4,1]{0,2,3,1:T(4,128)S(1)}, f32[19,18,4,1]{0,2,3,1:T(4,128)S(1)}, u32[]{:S(2)}, u32[]{:S(2)}) collective-permute-start(f32[19,18,4,1]{0,2,3,1:T(4,128)S(1)} %copy.502), channel_id=1, source_target_pairs={{1,0},{2,1},{3,2},{4,3},{5,4},{6,5},{7,6},{8,7},{9,8},{10,9},{11,1... | collective-permute-start | bytes 16424 | tf_op jit(solution)/shard_map/ppermute | solution.py:44
  87.9 2.1 collective-permute-start.7
  90.1 0.6 slice.385
  90.7 0.6 slice.383
  91.3 0.6 slice.386
  91.9 9.4 %collective-permute-done.7 = f32[19,18,4,1]{0,2,3,1:T(4,128)S(1)} collective-permute-done((f32[19,18,4,1]{0,2,3,1:T(4,128)S(1)}, f32[19,18,4,1]{0,2,3,1:T(4,128)S(1)}, u32[]{:S(2)}, u32[]{:S(2)}) %collective-permute-start.7) | collective-permute-done | bytes 5504 | tf_op jit(solution)/shard_map/ppermute | solution.py:41
  101.3 1.0 copy.505
  102.4 1.1 copy.503
  104.8 1.6 multiply_reduce_fusion
  107.7 111.4 %psum.16 = f32[]{:T(128)} all-reduce(f32[]{:T(128)S(6)} %add.2107), channel_id=1, replica_groups=mesh['gx'=16,'gy'=32] {'gx','gy'}, use_global_device_ids=true, to_apply=%region_1.2 | all-reduce | flops 1 | bytes 8 | tf_op jit(solution)/shard_map/psum | solution.py:121
  220.1 1.1 copy.527
  (201 shorter events, 7.3 us)
Async XLA Ops:
  1.4 15.7 %collective-permute-start.1 = (f32[19,1,4,128]{3,2,1,0:T(4,128)S(1)}, f32[19,1,4,128]{3,2,1,0:T(4,128)S(1)}, u32[]{:S(2)}, u32[]{:S(2)}) collective-permute-start(f32[19,1,4,128]{3,2,1,0:T(4,128)S(1)} %get-tuple-element.193), channel_id=1, source_target_pairs={{0,32},{32,64},{64,96},{96,128},{128,160},{160,192},{192,224},{224... | collective-permute-start | bytes 116744 | tf_op jit(solution)/shard_map/ppermute | solution.py:41
  6.0 8.0 %copy-start.48 = (bf16[2,3,16,4,128]{4,3,2,1,0:T(4,128)(2,1)S(1)}, bf16[2,3,16,4,128]{4,3,2,1,0:T(4,128)(2,1)}, u32[]{:S(2)}) copy-start(bf16[2,3,16,4,128]{4,3,2,1,0:T(4,128)(2,1)} %param.5) | copy-start | bytes 294916
  6.0 8.1 %copy-start.1 = (s32[18,16,4,128]{3,2,1,0:T(4,128)S(1)}, s32[18,16,4,128]{3,2,1,0:T(4,128)}, u32[]{:S(2)}) copy-start(s32[18,16,4,128]{3,2,1,0:T(4,128)} %param.7) | copy-start | bytes 1769476
  6.0 11.5 %collective-permute-start = (f32[19,1,4,128]{3,2,1,0:T(4,128)S(1)}, f32[19,1,4,128]{3,2,1,0:T(4,128)S(1)}, u32[]{:S(2)}, u32[]{:S(2)}) collective-permute-start(f32[19,1,4,128]{3,2,1,0:T(4,128)S(1)} %get-tuple-element.194), channel_id=1, source_target_pairs={{32,0},{64,32},{96,64},{128,96},{160,128},{192,160},{224,192},{256... | collective-permute-start | bytes 116744 | tf_op jit(solution)/shard_map/ppermute | solution.py:44
  15.0 2.2 copy-start
  20.4 25.3 %collective-permute-start.2 = (f32[19,18,4,1]{0,2,3,1:T(4,128)S(1)}, f32[19,18,4,1]{0,2,3,1:T(4,128)}, u32[]{:S(2)}, u32[]{:S(2)}) collective-permute-start(f32[19,18,4,1]{0,2,3,1:T(4,128)S(1)} %copy.538), channel_id=1, source_target_pairs={{1,0},{2,1},{3,2},{4,3},{5,4},{6,5},{7,6},{8,7},{9,8},{10,9},{11,1... | collective-permute-start | bytes 16424 | tf_op jit(solution)/shard_map/ppermute | solution.py:44
  31.3 13.4 %collective-permute-start.3 = (f32[19,18,4,1]{0,2,3,1:T(4,128)S(1)}, f32[19,18,4,1]{0,2,3,1:T(4,128)S(1)}, u32[]{:S(2)}, u32[]{:S(2)}) collective-permute-start(f32[19,18,4,1]{0,2,3,1:T(4,128)S(1)} %copy.541), channel_id=1, source_target_pairs={{0,1},{1,2},{2,3},{3,4},{4,5},{5,6},{6,7},{7,8},{8,9},{9,10},{10,1... | collective-permute-start | bytes 16424 | tf_op jit(solution)/shard_map/ppermute | solution.py:41
  47.6 0.8 copy-start.15
  47.6 0.8 copy-start.16
  47.6 0.8 copy-start.17
  47.6 0.8 copy-start.18
  47.7 0.8 copy-start.19
  47.7 0.8 copy-start.20
  47.7 0.9 copy-start.21
  47.7 0.9 copy-start.22
  47.7 0.9 copy-start.23
  47.7 0.9 copy-start.35
  47.7 0.9 copy-start.36
  47.7 0.9 copy-start.37
  47.7 0.9 copy-start.38
  47.7 0.9 copy-start.41
  47.8 0.9 copy-start.42
  47.8 0.9 copy-start.43
  47.8 0.9 copy-start.45
  47.9 0.8 copy-start.9
  47.9 0.8 copy-start.10
  47.9 0.8 copy-start.8
  48.0 0.8 copy-start.6
  48.0 0.8 copy-start.7
  48.0 0.8 copy-start.4
  48.0 0.8 copy-start.2
  48.0 0.8 copy-start.3
  58.3 17.9 %collective-permute-start.4 = (f32[19,1,4,128]{3,2,1,0:T(4,128)S(1)}, f32[19,1,4,128]{3,2,1,0:T(4,128)S(1)}, u32[]{:S(2)}, u32[]{:S(2)}) collective-permute-start(f32[19,1,4,128]{3,2,1,0:T(4,128)S(1)} %bitcast.557), channel_id=1, source_target_pairs={{32,0},{64,32},{96,64},{128,96},{160,128},{192,160},{224,192},{256... | collective-permute-start | bytes 116744 | tf_op jit(solution)/shard_map/ppermute | solution.py:44
  73.0 10.1 %collective-permute-start.5 = (f32[19,1,4,128]{3,2,1,0:T(4,128)S(1)}, f32[19,1,4,128]{3,2,1,0:T(4,128)S(1)}, u32[]{:S(2)}, u32[]{:S(2)}) collective-permute-start(f32[19,1,4,128]{3,2,1,0:T(4,128)S(1)} %bitcast.556), channel_id=1, source_target_pairs={{0,32},{32,64},{64,96},{96,128},{128,160},{160,192},{192,224},{224... | collective-permute-start | bytes 116744 | tf_op jit(solution)/shard_map/ppermute | solution.py:41
  84.8 17.6 %collective-permute-start.6 = (f32[19,18,4,1]{0,2,3,1:T(4,128)S(1)}, f32[19,18,4,1]{0,2,3,1:T(4,128)S(1)}, u32[]{:S(2)}, u32[]{:S(2)}) collective-permute-start(f32[19,18,4,1]{0,2,3,1:T(4,128)S(1)} %copy.502), channel_id=1, source_target_pairs={{1,0},{2,1},{3,2},{4,3},{5,4},{6,5},{7,6},{8,7},{9,8},{10,9},{11,1... | collective-permute-start | bytes 16424 | tf_op jit(solution)/shard_map/ppermute | solution.py:44
  87.9 13.4 %collective-permute-start.7 = (f32[19,18,4,1]{0,2,3,1:T(4,128)S(1)}, f32[19,18,4,1]{0,2,3,1:T(4,128)S(1)}, u32[]{:S(2)}, u32[]{:S(2)}) collective-permute-start(f32[19,18,4,1]{0,2,3,1:T(4,128)S(1)} %copy.504), channel_id=1, source_target_pairs={{0,1},{1,2},{2,3},{3,4},{4,5},{5,6},{6,7},{7,8},{8,9},{9,10},{10,1... | collective-permute-start | bytes 16424 | tf_op jit(solution)/shard_map/ppermute | solution.py:41
  103.6 0.8 copy-start.55
  103.6 0.8 copy-start.56
  103.6 0.8 copy-start.57
  103.6 0.8 copy-start.58
  103.6 0.8 copy-start.59
  103.6 0.8 copy-start.60
  103.6 0.8 copy-start.61
  103.6 0.8 copy-start.62
  103.6 0.8 copy-start.63
  104.0 0.8 copy-start.5
  104.0 0.8 copy-start.24
  106.4 112.7 %copy-start.34 = (f32[16,4,128]{2,0,1:T(8,128)S(1)}, f32[16,4,128]{2,0,1:T(8,128)}, u32[]{:S(2)}) copy-start(f32[16,4,128]{2,0,1:T(8,128)} %get-tuple-element.15) | copy-start | bytes 98308
  (28 other events, 21.9 us)
where the time goes:
time: 224 us; the launch traced here: 223 us
  blocking collectives  111 us (50%)
  starting transfers between devices  45.5 us (20%)
  waiting for transfers between devices  25.3 us (11%)
  local copies, waits for them, and re-layouts  23.7 us (11%)
  other arithmetic  12.3 us (5%)
  between operations  4.66 us (2%)
    psum x1, blocking collectives, per_device(): total = total + lax.psum(step_terms[adjoint_step], ('gx', 'gy'))  111 us
    ppermute x4, starting transfers between devices, with_halo(): lax.ppermute(lax.slice_in_dim(block, 0, width, axis=dim), axis, backward)  35 us
    ppermute x4, waiting for transfers between devices, with_halo(): lax.ppermute(lax.slice_in_dim(block, block.shape[dim] - width, None, axis...  25.3 us
    ppermute x4, starting transfers between devices, with_halo(): lax.ppermute(lax.slice_in_dim(block, block.shape[dim] - width, None, axis...  10.6 us
    unnamed x36, other arithmetic  7.93 us
    unnamed x141, local copies, waits for them, and re-layouts  5 us
  transfers between devices with their start and end apart: 8, of which 3 were waited for; matrix products, arithmetic and copies ran while one was open for 5% of the time, Pallas kernels for 0%

commit v1 on v0

--- a/solution.py
+++ b/solution.py
@@ -30,6 +30,12 @@
 lattice_weights = (1.0 / 3.0,) + (1.0 / 18.0,) * 6 + (1.0 / 36.0,) * 12
 relax_rate = 1.6
 drag_factor = 20.0
+
+
+def masks_remake(in_array, axis_id, a_name):
+    for h in (axis_id, a_name):
+        in_array = lax.psum(in_array, h)
+    return in_array
 
 
 def with_halo(block, sides, width):
@@ -118,7 +124,7 @@
         step_terms.append(jnp.sum(drag_field))
     total = jnp.zeros((), jnp.float32)
     for adjoint_step in range(STEPS):
-        total = total + lax.psum(step_terms[adjoint_step], ("gx", "gy"))
+        total = total + masks_remake(step_terms[adjoint_step], "gy", "gx")
     cell_count = rows_x * lax.axis_size("gx") * rows_y * lax.axis_size("gy") * levels
     scale = drag_factor / math.sqrt(cell_count)
     return (state, (-scale * total).reshape(1))

time: 224 us -> 302 us (1.35)
  blocking collectives: 111 us -> 190 us
    psum x1 -> x2, blocking collectives: 111 us -> 190 us  [masks_remake(): in_array = lax.psum(in_array, h)]
  transfers between devices with their start and end apart: 8 -> 8, of which waited for: 3 -> 3; matrix products, arithmetic and copies ran while one was open for 5% -> 4% of each run, Pallas kernels for 0% -> 0%
where the time goes in v1:
time: 302 us
  blocking collectives  190 us (63%)
  starting transfers between devices  45.5 us (15%)
  waiting for transfers between devices  25.3 us (8%)
  local copies, waits for them, and re-layouts  23.6 us (8%)
  other arithmetic  12.2 us (4%)
  between operations  4.61 us (2%)
    psum x2, blocking collectives, masks_remake(): in_array = lax.psum(in_array, h)  190 us
    ppermute x4, starting transfers between devices, with_halo(): lax.ppermute(lax.slice_in_dim(block, 0, width, axis=dim), axis, backward)  35 us
    ppermute x4, waiting for transfers between devices, with_halo(): lax.ppermute(lax.slice_in_dim(block, block.shape[dim] - width, None, axis...  25.3 us
    ppermute x4, starting transfers between devices, with_halo(): lax.ppermute(lax.slice_in_dim(block, block.shape[dim] - width, None, axis...  10.6 us
    unnamed x36, other arithmetic  7.84 us
  transfers between devices with their start and end apart: 8, of which 3 were waited for; matrix products, arithmetic and copies ran while one was open for 4% of the time, Pallas kernels for 0%

profile of v1, /device:TPU:1, one launch (start us, length us, event | category | flops | bytes accessed | tf_op | source)
XLA Modules:
  0.0 301.5 jit_solution(12882433771769041623)
XLA Ops:
  0.6 0.8 fusion.265
  1.4 4.6 %collective-permute-start.1 = (f32[19,1,4,128]{3,2,1,0:T(4,128)S(1)}, f32[19,1,4,128]{3,2,1,0:T(4,128)S(1)}, u32[]{:S(2)}, u32[]{:S(2)}) collective-permute-start(f32[19,1,4,128]{3,2,1,0:T(4,128)S(1)} %get-tuple-element.193), channel_id=1, source_target_pairs={{0,32},{32,64},{64,96},{96,128},{128,160},{160,192},{192,224},{224... | collective-permute-start | bytes 116744 | tf_op jit(solution)/shard_map/ppermute | solution.py:47
  6.0 6.2 %collective-permute-start = (f32[19,1,4,128]{3,2,1,0:T(4,128)S(1)}, f32[19,1,4,128]{3,2,1,0:T(4,128)S(1)}, u32[]{:S(2)}, u32[]{:S(2)}) collective-permute-start(f32[19,1,4,128]{3,2,1,0:T(4,128)S(1)} %get-tuple-element.194), channel_id=1, source_target_pairs={{32,0},{64,32},{96,64},{128,96},{160,128},{192,160},{224,192},{256... | collective-permute-start | bytes 116744 | tf_op jit(solution)/shard_map/ppermute | solution.py:50
  12.3 1.7 fusion.264
  14.1 0.8 fusion.266
  15.0 0.6 copy-done.67
  15.9 0.6 slice.360
  16.5 0.6 slice.361
  17.6 0.6 fusion.262
  18.2 0.6 fusion.261
  20.3 10.9 %collective-permute-start.2 = (f32[19,18,4,1]{0,2,3,1:T(4,128)S(1)}, f32[19,18,4,1]{0,2,3,1:T(4,128)}, u32[]{:S(2)}, u32[]{:S(2)}) collective-permute-start(f32[19,18,4,1]{0,2,3,1:T(4,128)S(1)} %copy.538), channel_id=1, source_target_pairs={{1,0},{2,1},{3,2},{4,3},{5,4},{6,5},{7,6},{8,7},{9,8},{10,9},{11,1... | collective-permute-start | bytes 16424 | tf_op jit(solution)/shard_map/ppermute | solution.py:50
  31.2 1.9 collective-permute-start.3
  33.3 0.6 slice.367
  33.9 0.6 slice.363
  34.5 0.6 slice.369
  35.1 0.6 slice.365
  35.7 8.9 %collective-permute-done.3 = f32[19,18,4,1]{0,2,3,1:T(4,128)S(1)} collective-permute-done((f32[19,18,4,1]{0,2,3,1:T(4,128)S(1)}, f32[19,18,4,1]{0,2,3,1:T(4,128)S(1)}, u32[]{:S(2)}, u32[]{:S(2)}) %collective-permute-start.3) | collective-permute-done | bytes 5504 | tf_op jit(solution)/shard_map/ppermute | solution.py:47
  44.7 1.0 copy.442
  45.7 1.8 copy.438
  48.8 1.7 multiply_reduce_fusion.1
  51.3 0.6 constant_dynamic-update-slice_fusion.17
  52.0 0.6 constant_dynamic-update-slice_fusion.16
  52.6 0.6 constant_dynamic-update-slice_fusion.15
  53.2 0.6 constant_dynamic-update-slice_fusion.14
  53.8 0.6 constant_dynamic-update-slice_fusion.13
  54.4 0.6 constant_dynamic-update-slice_fusion.12
  55.0 0.6 constant_dynamic-update-slice_fusion.11
  55.7 0.6 constant_dynamic-update-slice_fusion.10
  56.3 0.6 constant_dynamic-update-slice_fusion.9
  56.9 0.6 constant_dynamic-update-slice_fusion.8
  57.5 0.6 constant_dynamic-update-slice_fusion.7
  58.2 14.7 %collective-permute-start.4 = (f32[19,1,4,128]{3,2,1,0:T(4,128)S(1)}, f32[19,1,4,128]{3,2,1,0:T(4,128)S(1)}, u32[]{:S(2)}, u32[]{:S(2)}) collective-permute-start(f32[19,1,4,128]{3,2,1,0:T(4,128)S(1)} %bitcast.557), channel_id=1, source_target_pairs={{32,0},{64,32},{96,64},{128,96},{160,128},{192,160},{224,192},{256... | collective-permute-start | bytes 116744 | tf_op jit(solution)/shard_map/ppermute | solution.py:50
  72.9 1.9 collective-permute-start.5
  74.8 0.6 slice.382
  75.4 0.6 slice.381
  76.0 7.0 %collective-permute-done.5 = f32[19,1,4,128]{3,2,1,0:T(4,128)S(1)} collective-permute-done((f32[19,1,4,128]{3,2,1,0:T(4,128)S(1)}, f32[19,1,4,128]{3,2,1,0:T(4,128)S(1)}, u32[]{:S(2)}, u32[]{:S(2)}) %collective-permute-start.5) | collective-permute-done | bytes 38944 | tf_op jit(solution)/shard_map/ppermute | solution.py:47
  84.7 3.1 %collective-permute-start.6 = (f32[19,18,4,1]{0,2,3,1:T(4,128)S(1)}, f32[19,18,4,1]{0,2,3,1:T(4,128)S(1)}, u32[]{:S(2)}, u32[]{:S(2)}) collective-permute-start(f32[19,18,4,1]{0,2,3,1:T(4,128)S(1)} %copy.502), channel_id=1, source_target_pairs={{1,0},{2,1},{3,2},{4,3},{5,4},{6,5},{7,6},{8,7},{9,8},{10,9},{11,1... | collective-permute-start | bytes 16424 | tf_op jit(solution)/shard_map/ppermute | solution.py:50
  87.8 2.1 collective-permute-start.7
  90.0 0.6 slice.385
  90.6 0.6 slice.383
  91.2 0.6 slice.386
  91.8 9.4 %collective-permute-done.7 = f32[19,18,4,1]{0,2,3,1:T(4,128)S(1)} collective-permute-done((f32[19,18,4,1]{0,2,3,1:T(4,128)S(1)}, f32[19,18,4,1]{0,2,3,1:T(4,128)S(1)}, u32[]{:S(2)}, u32[]{:S(2)}) %collective-permute-start.7) | collective-permute-done | bytes 5504 | tf_op jit(solution)/shard_map/ppermute | solution.py:47
  101.2 1.0 copy.505
  102.3 1.1 copy.503
  104.7 1.6 multiply_reduce_fusion
  107.5 100.0 %psum.33 = f32[]{:T(128)} all-reduce(f32[]{:T(128)S(6)} %add.2111), channel_id=1, replica_groups=mesh['gx'=16,'gy'=32] {'gy'}, use_global_device_ids=true, to_apply=%region_1.2 | all-reduce | flops 1 | bytes 8 | tf_op jit(solution)/shard_map/psum | solution.py:37
  207.5 90.2 %psum.32 = f32[]{:T(128)} all-reduce(f32[]{:T(128)} %psum.33), channel_id=1, replica_groups=mesh['gx'=16,'gy'=32] {'gx'}, use_global_device_ids=true, to_apply=%region_2.3 | all-reduce | flops 1 | bytes 8 | tf_op jit(solution)/shard_map/psum | solution.py:37
  298.7 1.1 copy.527
  (202 shorter events, 7.9 us)
Async XLA Ops:
  1.4 15.7 %collective-permute-start.1 = (f32[19,1,4,128]{3,2,1,0:T(4,128)S(1)}, f32[19,1,4,128]{3,2,1,0:T(4,128)S(1)}, u32[]{:S(2)}, u32[]{:S(2)}) collective-permute-start(f32[19,1,4,128]{3,2,1,0:T(4,128)S(1)} %get-tuple-element.193), channel_id=1, source_target_pairs={{0,32},{32,64},{64,96},{96,128},{128,160},{160,192},{192,224},{224... | collective-permute-start | bytes 116744 | tf_op jit(solution)/shard_map/ppermute | solution.py:47
  6.0 8.0 %copy-start.48 = (bf16[2,3,16,4,128]{4,3,2,1,0:T(4,128)(2,1)S(1)}, bf16[2,3,16,4,128]{4,3,2,1,0:T(4,128)(2,1)}, u32[]{:S(2)}) copy-start(bf16[2,3,16,4,128]{4,3,2,1,0:T(4,128)(2,1)} %param.5) | copy-start | bytes 294916
  6.0 8.0 %copy-start.1 = (s32[18,16,4,128]{3,2,1,0:T(4,128)S(1)}, s32[18,16,4,128]{3,2,1,0:T(4,128)}, u32[]{:S(2)}) copy-start(s32[18,16,4,128]{3,2,1,0:T(4,128)} %param.7) | copy-start | bytes 1769476
  6.0 11.5 %collective-permute-start = (f32[19,1,4,128]{3,2,1,0:T(4,128)S(1)}, f32[19,1,4,128]{3,2,1,0:T(4,128)S(1)}, u32[]{:S(2)}, u32[]{:S(2)}) collective-permute-start(f32[19,1,4,128]{3,2,1,0:T(4,128)S(1)} %get-tuple-element.194), channel_id=1, source_target_pairs={{32,0},{64,32},{96,64},{128,96},{160,128},{192,160},{224,192},{256... | collective-permute-start | bytes 116744 | tf_op jit(solution)/shard_map/ppermute | solution.py:50
  14.9 2.2 copy-start
  20.3 25.3 %collective-permute-start.2 = (f32[19,18,4,1]{0,2,3,1:T(4,128)S(1)}, f32[19,18,4,1]{0,2,3,1:T(4,128)}, u32[]{:S(2)}, u32[]{:S(2)}) collective-permute-start(f32[19,18,4,1]{0,2,3,1:T(4,128)S(1)} %copy.538), channel_id=1, source_target_pairs={{1,0},{2,1},{3,2},{4,3},{5,4},{6,5},{7,6},{8,7},{9,8},{10,9},{11,1... | collective-permute-start | bytes 16424 | tf_op jit(solution)/shard_map/ppermute | solution.py:50
  31.2 13.4 %collective-permute-start.3 = (f32[19,18,4,1]{0,2,3,1:T(4,128)S(1)}, f32[19,18,4,1]{0,2,3,1:T(4,128)S(1)}, u32[]{:S(2)}, u32[]{:S(2)}) collective-permute-start(f32[19,18,4,1]{0,2,3,1:T(4,128)S(1)} %copy.541), channel_id=1, source_target_pairs={{0,1},{1,2},{2,3},{3,4},{4,5},{5,6},{6,7},{7,8},{8,9},{9,10},{10,1... | collective-permute-start | bytes 16424 | tf_op jit(solution)/shard_map/ppermute | solution.py:47
  47.6 0.8 copy-start.15
  47.6 0.8 copy-start.16
  47.6 0.8 copy-start.17
  47.6 0.8 copy-start.18
  47.6 0.8 copy-start.19
  47.6 0.8 copy-start.20
  47.6 0.9 copy-start.21
  47.6 0.9 copy-start.22
  47.6 0.9 copy-start.23
  47.7 0.9 copy-start.35
  47.7 0.9 copy-start.36
  47.7 0.9 copy-start.37
  47.7 0.9 copy-start.38
  47.7 0.9 copy-start.41
  47.7 0.9 copy-start.42
  47.7 0.9 copy-start.43
  47.7 0.9 copy-start.45
  47.9 0.8 copy-start.9
  47.9 0.8 copy-start.10
  47.9 0.8 copy-start.8
  47.9 0.8 copy-start.6
  47.9 0.8 copy-start.7
  47.9 0.8 copy-start.4
  48.0 0.8 copy-start.2
  48.0 0.8 copy-start.3
  58.2 17.9 %collective-permute-start.4 = (f32[19,1,4,128]{3,2,1,0:T(4,128)S(1)}, f32[19,1,4,128]{3,2,1,0:T(4,128)S(1)}, u32[]{:S(2)}, u32[]{:S(2)}) collective-permute-start(f32[19,1,4,128]{3,2,1,0:T(4,128)S(1)} %bitcast.557), channel_id=1, source_target_pairs={{32,0},{64,32},{96,64},{128,96},{160,128},{192,160},{224,192},{256... | collective-permute-start | bytes 116744 | tf_op jit(solution)/shard_map/ppermute | solution.py:50
  72.9 10.1 %collective-permute-start.5 = (f32[19,1,4,128]{3,2,1,0:T(4,128)S(1)}, f32[19,1,4,128]{3,2,1,0:T(4,128)S(1)}, u32[]{:S(2)}, u32[]{:S(2)}) collective-permute-start(f32[19,1,4,128]{3,2,1,0:T(4,128)S(1)} %bitcast.556), channel_id=1, source_target_pairs={{0,32},{32,64},{64,96},{96,128},{128,160},{160,192},{192,224},{224... | collective-permute-start | bytes 116744 | tf_op jit(solution)/shard_map/ppermute | solution.py:47
  84.7 17.6 %collective-permute-start.6 = (f32[19,18,4,1]{0,2,3,1:T(4,128)S(1)}, f32[19,18,4,1]{0,2,3,1:T(4,128)S(1)}, u32[]{:S(2)}, u32[]{:S(2)}) collective-permute-start(f32[19,18,4,1]{0,2,3,1:T(4,128)S(1)} %copy.502), channel_id=1, source_target_pairs={{1,0},{2,1},{3,2},{4,3},{5,4},{6,5},{7,6},{8,7},{9,8},{10,9},{11,1... | collective-permute-start | bytes 16424 | tf_op jit(solution)/shard_map/ppermute | solution.py:50
  87.8 13.4 %collective-permute-start.7 = (f32[19,18,4,1]{0,2,3,1:T(4,128)S(1)}, f32[19,18,4,1]{0,2,3,1:T(4,128)S(1)}, u32[]{:S(2)}, u32[]{:S(2)}) collective-permute-start(f32[19,18,4,1]{0,2,3,1:T(4,128)S(1)} %copy.504), channel_id=1, source_target_pairs={{0,1},{1,2},{2,3},{3,4},{4,5},{5,6},{6,7},{7,8},{8,9},{9,10},{10,1... | collective-permute-start | bytes 16424 | tf_op jit(solution)/shard_map/ppermute | solution.py:47
  103.4 0.8 copy-start.55
  103.4 0.8 copy-start.56
  103.5 0.8 copy-start.57
  103.5 0.8 copy-start.58
  103.5 0.8 copy-start.59
  103.5 0.8 copy-start.60
  103.5 0.8 copy-start.61
  103.5 0.8 copy-start.62
  103.5 0.8 copy-start.63
  103.8 0.8 copy-start.5
  103.8 0.8 copy-start.24
  106.2 191.4 %copy-start.34 = (f32[16,4,128]{2,0,1:T(8,128)S(1)}, f32[16,4,128]{2,0,1:T(8,128)}, u32[]{:S(2)}) copy-start(f32[16,4,128]{2,0,1:T(8,128)} %get-tuple-element.15) | copy-start | bytes 98308
  (28 other events, 21.9 us)
